TPU v7x, 32 devices: a whole 2x2x4 slice. The times are simulated.
32 devices in a mesh: row: 8 (over z, y), col: 4 (over x, core).
Axes of the slice: x: 2, y: 2, z: 4, core: 2. Of those that a mesh axis runs over, the one named last changes fastest.
Arguments:
- latents: bfloat16 [4, 1152, 4096], P(None, 'col', 'row'), may hold values from -6 to 6
- cond: bfloat16 [4, 1, 1152], P(None, None, 'row'), may hold values from -6 to 6
- w_ada: bfloat16 [2, 1152, 6, 1152], P(None, 'row', None, 'col'), may hold values from -0.1875 to 0.1875
- b_ada: bfloat16 [2, 6, 1152], P(None, None, 'col'), may hold values from -3 to 3
- w_qkv: bfloat16 [2, 1152, 3, 1152], P(None, 'row', None, 'col'), may hold values from -0.1875 to 0.1875
- b_qv: bfloat16 [2, 2, 1152], P(None, None, 'col'), may hold values from -3 to 3
- w_out: bfloat16 [2, 1152, 1152], P(None, 'row', 'col'), may hold values from -0.5 to 0.5
- b_out: bfloat16 [2, 1152], P(None, 'col'), may hold values from -2 to 2
- w_fc1: bfloat16 [2, 1152, 4608], P(None, 'row', 'col'), may hold values from -0.1875 to 0.1875
- b_fc1: bfloat16 [2, 4608], P(None, 'col'), may hold values from -3 to 3
- w_fc2: bfloat16 [2, 1152, 4608], P(None, 'row', 'col'), may hold values from -0.09375 to 0.09375
- b_fc2: bfloat16 [2, 1152], P(None, 'col'), may hold values from -2 to 2
- cotangent: bfloat16 [4, 1152, 4096], P(None, 'col', 'row'), may hold values from -6 to 6
Outputs:
- output: bfloat16 [4, 1152, 4096], P(None, 'col', 'row')
- grad_latents: float32 [4, 1152, 4096], P(None, 'col', 'row')
- grad_cond: float32 [4, 1, 1152], P(None, None, 'row')
- grad_w_ada: float32 [2, 1152, 6, 1152], P(None, 'row', None, 'col')
- grad_b_ada: float32 [2, 6, 1152], P(None, None, 'col')
- grad_w_qkv: float32 [2, 1152, 3, 1152], P(None, 'row', None, 'col')
- grad_b_qv: float32 [2, 2, 1152], P(None, None, 'col')
- grad_w_out: float32 [2, 1152, 1152], P(None, 'row', 'col')
- grad_b_out: float32 [2, 1152], P(None, 'col')
- grad_w_fc1: float32 [2, 1152, 4608], P(None, 'row', 'col')
- grad_b_fc1: float32 [2, 4608], P(None, 'col')
- grad_w_fc2: float32 [2, 1152, 4608], P(None, 'row', 'col')
- grad_b_fc2: float32 [2, 1152], P(None, 'col')
All inputs are finite; a program needn't handle non-finite values.
Results may differ from a plain program's by a relative error of at most 0.03.
Values may be sent and summed in bfloat16 or wider, within the bound.
No kernel may reach another device: no remote copies, remote signals or barrier semaphores. Data moves between devices by JAX's collectives and lax.ppermute only.
A program may use at most 320 MiB of HBM per device.

v0:
```python
import jax
import jax.numpy as jnp
from jax import lax
from jax.sharding import PartitionSpec as P

D = 1152
HD = 72
P_SIZE = 256
NF = 16
epsilon = 1e-06


def gelu_tanh(value):
    return jax.nn.gelu(value, approximate=True)


def contract_rows(left, right):
    return lax.dot_general(
        left, right, (((0,), (0,)), ((), ())), preferred_element_type=jnp.float32
    )


def contract_last(left, right):
    return lax.dot_general(
        left, right, (((1,), (1,)), ((), ())), preferred_element_type=jnp.float32
    )


def gather_features(value):
    return lax.all_gather(value, "col", axis=1, tiled=True)


def feature_sums(partial_value):
    return lax.psum_scatter(partial_value, "col", scatter_dimension=1, tiled=True)


def row_totals(first, second):
    return lax.psum((first, second), "col")


def fold_product(left, weight):
    return jnp.dot(
        left, lax.all_gather(weight, "row", axis=0, tiled=True), preferred_element_type=jnp.float32
    )


def map_product(left, weight):
    return contract_last(left, lax.all_gather(weight, "row", axis=0, tiled=True))


def norm_forward(stream):
    first, second = row_totals(jnp.sum(stream, 1), jnp.sum(stream * stream, 1))
    row_mean = first / D
    inverse = lax.rsqrt(second / D - row_mean * row_mean + epsilon)
    return ((stream - row_mean[:, None]) * inverse[:, None], inverse)


def norm_backward(grad_normed, normed, inverse):
    first, second = row_totals(jnp.sum(grad_normed, 1), jnp.sum(grad_normed * normed, 1))
    return inverse[:, None] * (grad_normed - first[:, None] / D - normed * second[:, None] / D)


def spread(vector, groups, tokens):
    width = vector.shape[-1]
    return jnp.broadcast_to(vector[:, None, :], (groups, tokens // groups, width)).reshape(
        tokens, width
    )


def group_sum(value, groups):
    return jnp.sum(value.reshape(groups, -1, value.shape[-1]), 1)


def split_heads(value, layout):
    return value.reshape(layout + (value.shape[1] // HD, HD))


def attention_scores(query_split, key_split):
    return jnp.einsum(
        "sqehd,skehd->sehqk", query_split, key_split, preferred_element_type=jnp.float32
    ) * HD ** (-0.5)


def attend_forward(queries, key_heads, value_heads, layout):
    tokens, width = queries.shape
    scores = attention_scores(split_heads(queries, layout), split_heads(key_heads, layout))
    largest = jnp.max(scores, -1, keepdims=True)
    powered = jnp.exp(scores - largest)
    total = jnp.sum(powered, -1, keepdims=True)
    soft_weights = (powered / total).astype(jnp.bfloat16)
    attended = jnp.einsum(
        "sehqk,skehd->sqehd",
        soft_weights,
        split_heads(value_heads, layout),
        preferred_element_type=jnp.float32,
    )
    return (attended.reshape(tokens, width), largest + jnp.log(total))


def attend_backward(queries, key_heads, value_heads, log_total, grad_out, layout):
    tokens, width = queries.shape
    query_split = split_heads(queries, layout)
    key_split = split_heads(key_heads, layout)
    value_split = split_heads(value_heads, layout)
    grad_split = split_heads(grad_out, layout)
    soft_weights = jnp.exp(attention_scores(query_split, key_split) - log_total)
    grad_weights = jnp.einsum(
        "sqehd,skehd->sehqk", grad_split, value_split, preferred_element_type=jnp.float32
    )
    grad_scores = (
        soft_weights * (grad_weights - jnp.sum(grad_weights * soft_weights, -1, keepdims=True))
    ).astype(jnp.bfloat16)
    factor = HD ** (-0.5)
    grad_query = (
        jnp.einsum("sehqk,skehd->sqehd", grad_scores, key_split, preferred_element_type=jnp.float32)
        * factor
    )
    grad_keys = (
        jnp.einsum(
            "sehqk,sqehd->skehd", grad_scores, query_split, preferred_element_type=jnp.float32
        )
        * factor
    )
    grad_values = jnp.einsum(
        "sehqk,sqehd->skehd",
        soft_weights.astype(jnp.bfloat16),
        grad_split,
        preferred_element_type=jnp.float32,
    )
    return (
        grad_query.reshape(tokens, width),
        grad_keys.reshape(tokens, width),
        grad_values.reshape(tokens, width),
    )


def block_forward(stream, modulate, weights, groups, layout):
    w_qkv, b_qv, w_out, b_out, w_fc1, b_fc1, w_fc2, b_fc2, out_local = weights
    tokens, width = stream.shape
    pieces = [spread(modulate[:, column], groups, tokens) for column in range(6)]
    normed, inverse = norm_forward(stream)
    hidden = (normed * (1.0 + pieces[1]) + pieces[0]).astype(jnp.bfloat16)
    hidden_all = gather_features(hidden)
    qv_bias = b_qv.astype(jnp.float32)
    biases = jnp.concatenate([qv_bias[0], jnp.zeros((width,), jnp.float32), qv_bias[1]])
    projected = (fold_product(hidden_all, w_qkv) + biases).astype(jnp.bfloat16)
    queries = projected[:, :width]
    key_heads = projected[:, width : 2 * width]
    value_heads = projected[:, 2 * width :]
    attended, log_total = attend_forward(queries, key_heads, value_heads, layout)
    attended_low = attended.astype(jnp.bfloat16)
    branch = feature_sums(map_product(attended_low, w_out)) + b_out.astype(jnp.float32)
    middle = stream + pieces[2] * branch
    normed_two, inverse_two = norm_forward(middle)
    hidden_two = (normed_two * (1.0 + pieces[4]) + pieces[3]).astype(jnp.bfloat16)
    hidden_two_all = gather_features(hidden_two)
    preact = fold_product(hidden_two_all, w_fc1) + b_fc1.astype(jnp.float32)
    activated = gelu_tanh(preact).astype(jnp.bfloat16)
    branch_two = feature_sums(map_product(activated, w_fc2)) + b_fc2.astype(jnp.float32)
    result = middle + pieces[5] * branch_two
    kept = (
        normed,
        inverse,
        hidden_all,
        queries,
        key_heads,
        value_heads,
        log_total,
        attended_low,
        branch,
        normed_two,
        inverse_two,
        hidden_two_all,
        preact,
        activated,
        branch_two,
    )
    return (result, kept)


def block_backward(grad, kept, modulate, weights, groups, layout):
    (
        normed,
        inverse,
        hidden_all,
        queries,
        key_heads,
        value_heads,
        log_total,
        attended_low,
        branch,
        normed_two,
        inverse_two,
        hidden_two_all,
        preact,
        activated,
        branch_two,
    ) = kept
    w_qkv, b_qv, w_out, b_out, w_fc1, b_fc1, w_fc2, b_fc2, out_local = weights
    tokens, width = grad.shape
    pieces = [spread(modulate[:, column], groups, tokens) for column in range(6)]
    grad_branch_two = (pieces[5] * grad).astype(jnp.bfloat16)
    grad_two_all = gather_features(grad_branch_two)
    grad_activated = fold_product(grad_two_all, w_fc2)
    grad_preact = jax.vjp(gelu_tanh, preact)[1](grad_activated)[0].astype(jnp.bfloat16)
    grad_hidden_two = feature_sums(map_product(grad_preact, w_fc1))
    grad_middle = grad + norm_backward(grad_hidden_two * (1.0 + pieces[4]), normed_two, inverse_two)
    grad_branch = (pieces[2] * grad_middle).astype(jnp.bfloat16)
    grad_branch_all = gather_features(grad_branch)
    grad_attended = fold_product(grad_branch_all, w_out).astype(jnp.bfloat16)
    grad_query, grad_keys, grad_values = attend_backward(
        queries, key_heads, value_heads, log_total, grad_attended, layout
    )
    grad_mixed = jnp.concatenate([grad_query, grad_keys, grad_values], 1).astype(jnp.bfloat16)
    grad_hidden = feature_sums(map_product(grad_mixed, w_qkv))
    grad_stream = grad_middle + norm_backward(grad_hidden * (1.0 + pieces[1]), normed, inverse)
    modulate_grad = jnp.stack(
        [
            group_sum(grad_hidden, groups),
            group_sum(grad_hidden * normed, groups),
            group_sum(grad_middle * branch, groups),
            group_sum(grad_hidden_two, groups),
            group_sum(grad_hidden_two * normed_two, groups),
            group_sum(grad * branch_two, groups),
        ],
        1,
    )
    weight_grads = (
        contract_rows(hidden_all, grad_mixed),
        contract_rows(grad_branch_all, attended_low),
        contract_rows(hidden_two_all, grad_preact),
        contract_rows(grad_two_all, activated),
    )
    mixed_float = grad_mixed.astype(jnp.float32)
    bias_grads = (
        jnp.stack([jnp.sum(mixed_float[:, :width], 0), jnp.sum(mixed_float[:, 2 * width :], 0)]),
        jnp.sum(grad_branch.astype(jnp.float32), 0),
        jnp.sum(grad_preact.astype(jnp.float32), 0),
        jnp.sum(grad_branch_two.astype(jnp.float32), 0),
    )
    return (grad_stream, weight_grads, bias_grads, modulate_grad)


def to_positions(value, frames_dev, row_count, pos_block):
    tokens, width = value.shape
    shaped = value.reshape(frames_dev, row_count, pos_block, width)
    moved = lax.all_to_all(shaped, "row", split_axis=1, concat_axis=0, tiled=True)
    return moved.reshape(tokens, width)


def to_frames(value, frames_dev, row_count, pos_block):
    tokens, width = value.shape
    shaped = value.reshape(frames_dev * row_count, 1, pos_block, width)
    moved = lax.all_to_all(
        shaped.astype(jnp.bfloat16), "row", split_axis=0, concat_axis=1, tiled=True
    ).astype(shaped.dtype)
    return moved.reshape(tokens, width)


def shards(
    latents, cond, w_ada, b_ada, w_qkv, b_qv, w_out, b_out, w_fc1, b_fc1, w_fc2, b_fc2, cotangent
):
    batches, width, tokens = latents.shape
    lat_count = cond.shape[1]
    row_count = lax.axis_size("row")
    frames_dev = tokens // P_SIZE
    pos_block = tokens // (lat_count * NF)
    spatial = (frames_dev, P_SIZE, 1)
    temporal = (lat_count, NF, pos_block)
    cond_float = cond.astype(jnp.float32)
    cond_low = jax.nn.silu(cond_float).astype(jnp.bfloat16)
    mod_partial = jnp.einsum("mlr,brjk->mlbjk", cond_low, w_ada, preferred_element_type=jnp.float32)
    mod_all = lax.psum(mod_partial, "row") + b_ada.astype(jnp.float32)[None, None]
    qkv_weight, out_weight, fc1_weight, fc2_weight = (w_qkv, w_out, w_fc1, w_fc2)
    out_locals = [None, None]
    block_weights = [
        (
            qkv_weight[which].reshape(qkv_weight.shape[1], -1),
            b_qv[which],
            out_weight[which],
            b_out[which],
            fc1_weight[which],
            b_fc1[which],
            fc2_weight[which],
            b_fc2[which],
            out_locals[which],
        )
        for which in range(2)
    ]
    lat_here = lax.axis_index("row") * frames_dev // NF
    onehot = (jnp.arange(lat_count) == lat_here).astype(jnp.float32)
    outputs = []
    grad_inputs = []
    mod_grads = []
    weight_totals = None
    bias_totals = None
    for batch_index in range(batches):
        mod_batch = mod_all[batch_index]
        mod_space = lax.dynamic_slice_in_dim(mod_batch[:, 0], lat_here, 1, 0)
        mod_time = mod_batch[:, 1]
        first_out, kept_space = block_forward(
            latents[batch_index].T.astype(jnp.float32), mod_space, block_weights[0], 1, spatial
        )
        second_in = to_positions(first_out, frames_dev, row_count, pos_block)
        second_out, kept_time = block_forward(
            second_in, mod_time, block_weights[1], lat_count, temporal
        )
        outputs.append(
            to_frames(second_out, frames_dev, row_count, pos_block).astype(jnp.bfloat16).T
        )
        grad_top = to_positions(
            cotangent[batch_index].T.astype(jnp.float32), frames_dev, row_count, pos_block
        )
        grad_mid, weights_time, biases_time, mod_grad_time = block_backward(
            grad_top, kept_time, mod_time, block_weights[1], lat_count, temporal
        )
        grad_low = to_frames(grad_mid, frames_dev, row_count, pos_block)
        grad_first, weights_space, biases_space, mod_grad_space = block_backward(
            grad_low, kept_space, mod_space, block_weights[0], 1, spatial
        )
        grad_inputs.append(grad_first.T)
        mod_grads.append(jnp.stack([onehot[:, None, None] * mod_grad_space, mod_grad_time], 1))
        terms = tuple(
            (jnp.stack([weights_space[column], weights_time[column]]) for column in range(4))
        )
        bias_terms = tuple(
            (jnp.stack([biases_space[column], biases_time[column]]) for column in range(4))
        )
        terms = (
            lax.psum_scatter(
                terms[0].astype(jnp.bfloat16), "row", scatter_dimension=1, tiled=True
            ).astype(jnp.float32),
            lax.psum_scatter(
                terms[1].astype(jnp.bfloat16), "row", scatter_dimension=1, tiled=True
            ).astype(jnp.float32),
            lax.psum_scatter(
                terms[2].astype(jnp.bfloat16), "row", scatter_dimension=1, tiled=True
            ).astype(jnp.float32),
            lax.psum_scatter(
                terms[3].astype(jnp.bfloat16), "row", scatter_dimension=1, tiled=True
            ).astype(jnp.float32),
        )
        if weight_totals is None:
            weight_totals = terms
            bias_totals = bias_terms
        else:
            weight_totals = jax.tree.map(jnp.add, weight_totals, terms)
            bias_totals = jax.tree.map(jnp.add, bias_totals, bias_terms)
    mod_grad_all, grad_bias_qv, grad_bias_out, grad_bias_fc1, grad_bias_fc2 = lax.psum(
        (jnp.stack(mod_grads), bias_totals[0], bias_totals[1], bias_totals[2], bias_totals[3]),
        "row",
    )
    mod_grad_low = mod_grad_all.astype(jnp.bfloat16)
    grad_bias_ada = jnp.sum(mod_grad_low.astype(jnp.float32), (0, 1))
    grad_weight_ada = jnp.einsum(
        "mlr,mlbjk->brjk", cond_low, mod_grad_low, preferred_element_type=jnp.float32
    )
    cond_partial = jnp.einsum(
        "mlbjk,brjk->mlr", mod_grad_low, w_ada, preferred_element_type=jnp.float32
    )
    cond_total = lax.psum(cond_partial, "col")
    sigmoid_cond = jax.nn.sigmoid(cond_float)
    grad_condition = cond_total * sigmoid_cond * (1.0 + cond_float * (1.0 - sigmoid_cond))
    grad_weight_qkv = weight_totals[0].reshape(2, weight_totals[0].shape[1], 3, width)
    return (
        jnp.stack(outputs),
        jnp.stack(grad_inputs),
        grad_condition,
        grad_weight_ada,
        grad_bias_ada,
        grad_weight_qkv,
        grad_bias_qv,
        weight_totals[1],
        grad_bias_out,
        weight_totals[2],
        grad_bias_fc1,
        weight_totals[3],
        grad_bias_fc2,
    )


def solution(mesh):
    placed = (
        P(None, "col", "row"),
        P(None, None, "row"),
        P(None, "row", None, "col"),
        P(None, None, "col"),
        P(None, "row", None, "col"),
        P(None, None, "col"),
        P(None, "row", "col"),
        P(None, "col"),
        P(None, "row", "col"),
        P(None, "col"),
        P(None, "row", "col"),
        P(None, "col"),
        P(None, "col", "row"),
    )
    return jax.shard_map(
        shards,
        mesh=mesh,
        in_specs=placed,
        out_specs=(
            P(None, "col", "row"),
            P(None, "col", "row"),
            P(None, None, "row"),
            P(None, "row", None, "col"),
            P(None, None, "col"),
            P(None, "row", None, "col"),
            P(None, None, "col"),
            P(None, "row", "col"),
            P(None, "col"),
            P(None, "row", "col"),
            P(None, "col"),
            P(None, "row", "col"),
            P(None, "col"),
        ),
        check_vma=False,
    )
```

profile of v0, /device:TPU:0, one launch (start us, length us, event | category | flops | bytes accessed | tf_op | source)
XLA Modules:
  0.0 4143.3 jit_solution(4381274286340281583)
XLA Ops:
  12.1 39.9 psum.497
  64.3 34.9 all-gather
  187.7 43.8 %all-gather.113.cloned.1.call-done = bf16[1,1152,1152]{2,1,0:T(8,128)(2,1)} async-done(((bf16[1,144,1152]{2,1,0:T(8,128)(2,1)}), bf16[1,1152,1152]{2,1,0:T(8,128)(2,1)}) %all-gather.113.cloned.1.call-update) | async-done | bytes 2654224 | tf_op jit(solution)/shard_map/all_gather | solution.py:43
  254.9 52.5 %all-gather.115.cloned.1.call-done = bf16[1,1152,1152]{2,1,0:T(8,128)(2,1)} async-done(((bf16[1,144,1152]{2,1,0:T(8,128)(2,1)}), bf16[1,1152,1152]{2,1,0:T(8,128)(2,1)}) %all-gather.115.cloned.1.call-update) | async-done | bytes 2654224 | tf_op jit(solution)/shard_map/all_gather | solution.py:48
  402.4 34.4 all-gather.3
  509.7 37.8 all_to_all.228
  596.2 57.3 %all-gather.119.cloned.1.call-done = bf16[1,1152,1152]{2,1,0:T(8,128)(2,1)} async-done(((bf16[1,144,1152]{2,1,0:T(8,128)(2,1)}), bf16[1,1152,1152]{2,1,0:T(8,128)(2,1)}) %all-gather.119.cloned.1.call-update) | async-done | bytes 2654224 | tf_op jit(solution)/shard_map/all_gather | solution.py:48
  782.4 33.1 reduce-scatter.75.cloned.1.call-done
  877.6 33.1 reduce-scatter.77.cloned.1.call-done
  955.0 32.3 reduce-scatter.79.cloned.1.call-done
  1094.2 35.6 reduce-scatter.65.cloned.1.call-done
  1129.8 35.6 reduce-scatter.49.cloned.1.call-done
  1274.2 35.5 reduce-scatter.59.cloned.1.call-done
  1309.7 35.8 reduce-scatter.67.cloned.1.call-done
  1529.6 35.7 reduce-scatter.61.cloned.1.call-done
  1565.2 35.6 reduce-scatter.53.cloned.1.call-done
  1816.7 33.5 reduce-scatter.81.cloned.1.call-done
  1921.5 35.6 reduce-scatter.55.cloned.1.call-done
  2053.9 32.5 reduce-scatter.83.cloned.1.call-done
  2088.3 33.7 reduce-scatter.99.cloned.1.call-done
  2281.3 33.7 reduce-scatter.85.cloned.1.call-done
  2317.0 33.5 reduce-scatter.101.cloned.1.call-done
  2714.9 52.5 %reduce-scatter.115.cloned.1.call-done = bf16[2,144,1152]{2,1,0:T(8,128)(2,1)} async-done(((bf16[2,1152,1152]{2,1,0:T(8,128)(2,1)}), bf16[2,144,1152]{2,1,0:T(8,128)(2,1)}) %reduce-scatter.115.cloned.1.call-update) | async-done | bytes 663568 | tf_op jit(solution)/shard_map/reduce_scatter | solution.py:339
  2767.4 107.2 %reduce-scatter.117.cloned.1.call-done = bf16[2,144,1152]{2,1,0:T(8,128)(2,1)} async-done(((bf16[2,1152,1152]{2,1,0:T(8,128)(2,1)}), bf16[2,144,1152]{2,1,0:T(8,128)(2,1)}) %reduce-scatter.117.cloned.1.call-update) | async-done | bytes 663568 | tf_op jit(solution)/shard_map/reduce_scatter | solution.py:339
  2877.8 104.0 %reduce-scatter.105.cloned.1.call-done = bf16[2,144,1152]{2,1,0:T(8,128)(2,1)} async-done(((bf16[2,1152,1152]{2,1,0:T(8,128)(2,1)}), bf16[2,144,1152]{2,1,0:T(8,128)(2,1)}) %reduce-scatter.105.cloned.1.call-update) | async-done | bytes 663568 | tf_op jit(solution)/shard_map/reduce_scatter | solution.py:336
  2981.7 107.1 %reduce-scatter.109.cloned.1.call-done = bf16[2,144,1152]{2,1,0:T(8,128)(2,1)} async-done(((bf16[2,1152,1152]{2,1,0:T(8,128)(2,1)}), bf16[2,144,1152]{2,1,0:T(8,128)(2,1)}) %reduce-scatter.109.cloned.1.call-update) | async-done | bytes 663568 | tf_op jit(solution)/shard_map/reduce_scatter | solution.py:336
  3088.9 107.1 %reduce-scatter.107.cloned.1.call-done = bf16[2,144,1152]{2,1,0:T(8,128)(2,1)} async-done(((bf16[2,1152,1152]{2,1,0:T(8,128)(2,1)}), bf16[2,144,1152]{2,1,0:T(8,128)(2,1)}) %reduce-scatter.107.cloned.1.call-update) | async-done | bytes 663568 | tf_op jit(solution)/shard_map/reduce_scatter | solution.py:336
  3196.0 107.2 %reduce-scatter.111.cloned.1.call-done = bf16[2,144,1152]{2,1,0:T(8,128)(2,1)} async-done(((bf16[2,1152,1152]{2,1,0:T(8,128)(2,1)}), bf16[2,144,1152]{2,1,0:T(8,128)(2,1)}) %reduce-scatter.111.cloned.1.call-update) | async-done | bytes 663568 | tf_op jit(solution)/shard_map/reduce_scatter | solution.py:336
  3338.5 36.2 reduce-scatter.87.cloned.1.call-done
  3374.7 35.8 reduce-scatter.103.cloned.1.call-done
  3413.5 40.3 all-reduce.8
  3473.1 650.4 %all-reduce.27.cloned.1.call-done = (bf16[2,1152,864]{2,0,1:T(2,128)(2,1)}, bf16[2,1152,864]{2,0,1:T(2,128)(2,1)}, bf16[2,1152,864]{2,0,1:T(2,128)(2,1)}, bf16[2...) async-done(((bf16[2,1152,864]{2,0,1:T(2,128)(2,1)}, ...) | async-done | bytes 21233680
  (1738 shorter events, 1958.1 us)
Async XLA Ops:
  63.4 110.1 %reduce-scatter.41.cloned.1.call-start = ((), (), s32[]{:S(2)}) async-start(), calls=%async_computation.58 | async-start | bytes 2949120 | tf_op jit(solution)/shard_map/reduce_scatter | solution.py:34
  143.9 105.7 %all-gather.49.cloned.1.call-start = ((), (), s32[]{:S(2)}) async-start(), calls=%async_computation.59 | async-start | bytes 1474560 | tf_op jit(solution)/shard_map/all_gather | solution.py:30
  184.7 122.7 %all-gather.115.cloned.1.call-start = ((), (), s32[]{:S(2)}) async-start(), calls=%async_computation.131 | async-start | bytes 2985984 | tf_op jit(solution)/shard_map/all_gather | solution.py:48
  186.8 158.1 %reduce-scatter.43.cloned.1.call-start = ((), (), s32[]{:S(2)}) async-start(), calls=%async_computation.60 | async-start | bytes 2949120 | tf_op jit(solution)/shard_map/reduce_scatter | solution.py:34
  313.2 123.5 %all-gather.53.cloned.1.call-start = ((), (), s32[]{:S(2)}) async-start(), calls=%async_computation.62 | async-start | bytes 2322432 | tf_op jit(solution)/shard_map/all_gather | solution.py:43
  463.6 112.9 %all-gather.55.cloned.1.call-start = ((), (), s32[]{:S(2)}) async-start(), calls=%async_computation.64 | async-start | bytes 1474560 | tf_op jit(solution)/shard_map/all_gather | solution.py:30
  552.2 144.2 %reduce-scatter.73.cloned.1.call-start = ((), (), s32[]{:S(2)}) async-start(), calls=%async_computation.91 | async-start | bytes 2949120 | tf_op jit(solution)/shard_map/reduce_scatter | solution.py:34
  1054.8 110.6 %reduce-scatter.49.cloned.1.call-start = ((), (), s32[]{:S(2)}) async-start(), calls=%async_computation.67 | async-start | bytes 2949120 | tf_op jit(solution)/shard_map/reduce_scatter | solution.py:34
  1074.5 124.7 %all-gather.59.cloned.1.call-start = ((), (), s32[]{:S(2)}) async-start(), calls=%async_computation.68 | async-start | bytes 1474560 | tf_op jit(solution)/shard_map/all_gather | solution.py:30
  1227.5 118.0 %reduce-scatter.67.cloned.1.call-start = ((), (), s32[]{:S(2)}) async-start(), calls=%async_computation.85 | async-start | bytes 2949120 | tf_op jit(solution)/shard_map/reduce_scatter | solution.py:34
  1521.7 196.3 %all-gather.79.cloned.1.call-start = ((), (), s32[]{:S(2)}) async-start(), calls=%async_computation.88 | async-start | bytes 1474560 | tf_op jit(solution)/shard_map/all_gather | solution.py:30
  1618.4 105.0 %all-gather.105.cloned.1.call-start = ((), (), s32[]{:S(2)}) async-start(), calls=%async_computation.114 | async-start | bytes 1474560 | tf_op jit(solution)/shard_map/all_gather | solution.py:30
  1767.5 118.3 %reduce-scatter.63.cloned.1.call-start = ((), (), s32[]{:S(2)}) async-start(), calls=%async_computation.81 | async-start | bytes 2949120 | tf_op jit(solution)/shard_map/reduce_scatter | solution.py:34
  1773.4 148.1 %reduce-scatter.71.cloned.1.call-start = ((), (), s32[]{:S(2)}) async-start(), calls=%async_computation.89 | async-start | bytes 2949120 | tf_op jit(solution)/shard_map/reduce_scatter | solution.py:34
  1779.2 177.9 %reduce-scatter.55.cloned.1.call-start = ((), (), s32[]{:S(2)}) async-start(), calls=%async_computation.73 | async-start | bytes 2949120 | tf_op jit(solution)/shard_map/reduce_scatter | solution.py:34
  1785.1 191.6 %all-gather.99.cloned.1.call-start = ((), (), s32[]{:S(2)}) async-start(), calls=%async_computation.108 | async-start | bytes 1474560 | tf_op jit(solution)/shard_map/all_gather | solution.py:30
  1889.4 116.9 %all-gather.91.cloned.1.call-start = ((), (), s32[]{:S(2)}) async-start(), calls=%async_computation.100 | async-start | bytes 1474560 | tf_op jit(solution)/shard_map/all_gather | solution.py:30
  2235.8 114.7 %reduce-scatter.101.cloned.1.call-start = ((), (), s32[]{:S(2)}) async-start(), calls=%async_computation.119 | async-start | bytes 2949120 | tf_op jit(solution)/shard_map/reduce_scatter | solution.py:34
  2254.9 188.9 %all-gather.103.cloned.1.call-start = ((), (), s32[]{:S(2)}) async-start(), calls=%async_computation.112 | async-start | bytes 1474560 | tf_op jit(solution)/shard_map/all_gather | solution.py:30
  2368.7 136.1 %all-gather.111.cloned.1.call-start = ((), (), s32[]{:S(2)}) async-start(), calls=%async_computation.120 | async-start | bytes 1474560 | tf_op jit(solution)/shard_map/all_gather | solution.py:30
  2371.7 343.2 %reduce-scatter.113.cloned.1.call-start = ((), (), s32[]{:S(2)}) async-start(), calls=%async_computation.126 | async-start | bytes 5971968 | tf_op jit(solution)/shard_map/reduce_scatter | solution.py:339
  2380.7 334.3 %reduce-scatter.119.cloned.1.call-start = ((), (), s32[]{:S(2)}) async-start(), calls=%async_computation.129 | async-start | bytes 5971968 | tf_op jit(solution)/shard_map/reduce_scatter | solution.py:339
  2390.4 377.0 %reduce-scatter.115.cloned.1.call-start = ((), (), s32[]{:S(2)}) async-start(), calls=%async_computation.127 | async-start | bytes 5971968 | tf_op jit(solution)/shard_map/reduce_scatter | solution.py:339
  2400.2 474.4 %reduce-scatter.117.cloned.1.call-start = ((), (), s32[]{:S(2)}) async-start(), calls=%async_computation.128 | async-start | bytes 5971968 | tf_op jit(solution)/shard_map/reduce_scatter | solution.py:339
  2409.8 571.9 %reduce-scatter.105.cloned.1.call-start = ((), (), s32[]{:S(2)}) async-start(), calls=%async_computation.122 | async-start | bytes 5971968 | tf_op jit(solution)/shard_map/reduce_scatter | solution.py:336
  2418.1 670.7 %reduce-scatter.109.cloned.1.call-start = ((), (), s32[]{:S(2)}) async-start(), calls=%async_computation.124 | async-start | bytes 5971968 | tf_op jit(solution)/shard_map/reduce_scatter | solution.py:336
  2426.4 769.6 %reduce-scatter.107.cloned.1.call-start = ((), (), s32[]{:S(2)}) async-start(), calls=%async_computation.123 | async-start | bytes 5971968 | tf_op jit(solution)/shard_map/reduce_scatter | solution.py:336
  2434.9 868.3 %reduce-scatter.111.cloned.1.call-start = ((), (), s32[]{:S(2)}) async-start(), calls=%async_computation.125 | async-start | bytes 5971968 | tf_op jit(solution)/shard_map/reduce_scatter | solution.py:336
  2443.1 895.4 %reduce-scatter.95.cloned.1.call-start = ((), (), s32[]{:S(2)}) async-start(), calls=%async_computation.113 | async-start | bytes 2949120 | tf_op jit(solution)/shard_map/reduce_scatter | solution.py:34
  2457.5 917.2 %reduce-scatter.87.cloned.1.call-start = ((), (), s32[]{:S(2)}) async-start(), calls=%async_computation.105 | async-start | bytes 2949120 | tf_op jit(solution)/shard_map/reduce_scatter | solution.py:34
  2472.0 938.5 %reduce-scatter.103.cloned.1.call-start = ((), (), s32[]{:S(2)}) async-start(), calls=%async_computation.121 | async-start | bytes 2949120 | tf_op jit(solution)/shard_map/reduce_scatter | solution.py:34
  2518.6 1604.9 %all-reduce.27.cloned.1.call-start = ((), (), s32[]{:S(2)}) async-start(), calls=%async_computation.134 | async-start | bytes 47185920
  (471 other events, 21171.2 us)
Sparse Core Ops, SparseCore 0:
  79.3 50.9 all-gather.46
  176.4 55.0 all-gather.112
  252.4 55.0 all-gather.114
  347.7 60.2 all-gather.52
  496.8 61.8 all-gather.116
  598.4 55.0 all-gather.118
  698.7 33.0 reduce-scatter.46
  954.2 33.0 reduce-scatter.78
  1061.1 33.0 reduce-scatter.56
  1132.3 33.0 reduce-scatter.48
  1241.1 33.0 reduce-scatter.50
  1276.6 33.0 reduce-scatter.58
  1312.4 33.0 reduce-scatter.66
  1532.1 33.0 reduce-scatter.60
  1567.8 33.0 reduce-scatter.52
  1746.0 33.0 reduce-scatter.96
  1781.5 33.0 reduce-scatter.88
  1852.8 33.0 reduce-scatter.62
  2017.6 33.0 reduce-scatter.90
  2053.3 33.0 reduce-scatter.82
  2246.3 33.0 reduce-scatter.92
  2426.3 103.6 reduce-scatter.112
  2534.2 116.8 reduce-scatter.118
  2655.0 112.3 reduce-scatter.114
  2771.6 103.0 reduce-scatter.116
  2878.6 103.0 reduce-scatter.104
  2985.8 103.0 reduce-scatter.108
  3092.9 103.0 reduce-scatter.106
  3200.1 103.0 reduce-scatter.110
  3341.6 33.0 reduce-scatter.86
  3377.4 33.0 reduce-scatter.102
  3416.2 707.2 all-reduce.26
  (47 shorter events, 1036.3 us)
where the time goes:
time: 4160 us; the launch traced here: 4140 us
  waiting for transfers between devices  2730 us (66%)
  blocking collectives  403 us (10%)
  matrix products  393 us (9%)
  local copies, waits for them, and re-layouts  330 us (8%)
  other arithmetic  212 us (5%)
  starting transfers between devices  57.1 us (1%)
    reduce_scatter x32, waiting for transfers between devices, feature_sums(): lax.psum_scatter(partial_value, 'col', scatter_dimension=1, tiled=True)  917 us
    unnamed x80, waiting for transfers between devices  655 us
    reduce_scatter x4, waiting for transfers between devices, shards(): lax.psum_scatter(terms[2].astype(jnp.bfloat16), 'row', scatter_dimension=...  425 us
    all_gather x32, waiting for transfers between devices, gather_features(): return lax.all_gather(value, 'col', axis=1, tiled=True)  221 us
    reduce_scatter x4, waiting for transfers between devices, shards(): lax.psum_scatter(terms[3].astype(jnp.bfloat16), 'row', scatter_dimension=...  160 us
    dot_general x32, matrix products, fold_product(): jnp.dot(left, lax.all_gather(weight, 'row', axis=0, tiled=True), preferre...  143 us
    psum x15, blocking collectives, row_totals(): return lax.psum((first, second), 'col')  126 us
    dot_general x32, matrix products, contract_last(): lax.dot_general(left, right, (((1,), (1,)), ((), ())), preferred_element_...  116 us
  transfers between devices with their start and end apart: 90, of which 71 were waited for; matrix products, arithmetic and copies ran while one was open for 17% of the time, Pallas kernels for 0%

commit v1 on v0

--- a/solution.py
+++ b/solution.py
@@ -10,6 +10,19 @@
 epsilon = 1e-06
 
 
+def collect(x, axis, dim):
+    ways = lax.axis_size(axis)
+    up = [(d, (d + 1) % ways) for d in range(ways)]
+    down = [(d, (d - 1) % ways) for d in range(ways)]
+    earlier, later = ([x], [x])
+    for _ in range(ways // 2):
+        earlier.append(lax.ppermute(earlier[-1], axis, up))
+    for _ in range((ways - 1) // 2):
+        later.append(lax.ppermute(later[-1], axis, down))
+    line = jnp.concatenate([*earlier[::-1], *later[1:]], axis=dim)
+    return jnp.roll(line, (lax.axis_index(axis) - ways // 2) * x.shape[dim], axis=dim)
+
+
 def gelu_tanh(value):
     return jax.nn.gelu(value, approximate=True)
 
@@ -45,7 +58,7 @@
 
 
 def map_product(left, weight):
-    return contract_last(left, lax.all_gather(weight, "row", axis=0, tiled=True))
+    return contract_last(left, collect(weight, "row", 0))
 
 
 def norm_forward(stream):

time: 4160 us -> 4310 us (1.036)
  starting transfers between devices: 57.1 us -> 183 us
  waiting for transfers between devices: 2730 us -> 2680 us
  local copies, waits for them, and re-layouts: 330 us -> 378 us
    ppermute x0 -> x56, waiting for transfers between devices: none -> 261 us  [the longest x32 132 us: collect(): earlier.append(lax.ppermute(earlier[-1], axis, up))]
    ppermute x0 -> x56, starting transfers between devices: none -> 121 us  [the longest x24 92.5 us: collect(): later.append(lax.ppermute(later[-1], axis, down))]
    reduce_scatter x32, waiting for transfers between devices: 917 us -> 805 us  [feature_sums(): lax.psum_scatter(partial_value, 'col', scatter_dimension=1, tiled=True)]
    all_gather x2 -> x0, waiting for transfers between devices: 110 us -> none  [map_product(): lax.all_gather(weight, 'row', axis=0, tiled=True)]
    all_gather x32, waiting for transfers between devices: 221 us -> 142 us  [gather_features(): return lax.all_gather(value, 'col', axis=1, tiled=True)]
    unnamed x904 -> x991, local copies, waits for them, and re-layouts: 61 us -> 105 us
    all_to_all x7 -> x8, waiting for transfers between devices: 79.9 us -> 89.6 us  [to_frames(): lax.all_to_all(shaped.astype(jnp.bfloat16), 'row', split_axis=0, concat_a...]
  transfers between devices with their start and end apart: 90 -> 147, of which waited for: 71 -> 99; matrix products, arithmetic and copies ran while one was open for 17% -> 19% of each run, Pallas kernels for 0% -> 0%
where the time goes in v1:
time: 4310 us; the launch traced here: 4290 us
  waiting for transfers between devices  2680 us (62%)
  blocking collectives  390 us (9%)
  matrix products  387 us (9%)
  local copies, waits for them, and re-layouts  378 us (9%)
  other arithmetic  251 us (6%)
  starting transfers between devices  183 us (4%)
    reduce_scatter x32, waiting for transfers between devices, feature_sums(): lax.psum_scatter(partial_value, 'col', scatter_dimension=1, tiled=True)  805 us
    unnamed x80, waiting for transfers between devices  655 us
    reduce_scatter x4, waiting for transfers between devices, shards(): lax.psum_scatter(terms[2].astype(jnp.bfloat16), 'row', scatter_dimension=...  425 us
    reduce_scatter x4, waiting for transfers between devices, shards(): lax.psum_scatter(terms[3].astype(jnp.bfloat16), 'row', scatter_dimension=...  160 us
    dot_general x32, matrix products, fold_product(): jnp.dot(left, lax.all_gather(weight, 'row', axis=0, tiled=True), preferre...  142 us
    all_gather x32, waiting for transfers between devices, gather_features(): return lax.all_gather(value, 'col', axis=1, tiled=True)  142 us
    ppermute x32, waiting for transfers between devices, collect(): earlier.append(lax.ppermute(earlier[-1], axis, up))  132 us
    ppermute x24, waiting for transfers between devices, collect(): later.append(lax.ppermute(later[-1], axis, down))  129 us
  transfers between devices with their start and end apart: 147, of which 99 were waited for; matrix products, arithmetic and copies ran while one was open for 19% of the time, Pallas kernels for 0%

profile of v1, /device:TPU:0, one launch (start us, length us, event | category | flops | bytes accessed | tf_op | source)
XLA Modules:
  0.0 4289.7 jit_solution(4388474331109511098)
XLA Ops:
  12.1 39.9 psum.497
  433.9 32.6 reduce-scatter.45.cloned.1.call-done
  481.8 38.4 all_to_all.228
  625.8 34.0 all-gather.117.cloned.1.call-done
  763.3 36.3 all-gather.3
  842.9 33.7 reduce-scatter.75.cloned.1.call-done
  1040.1 34.5 all-gather.5
  1101.2 32.4 reduce-scatter.79.cloned.1.call-done
  1240.4 35.6 reduce-scatter.65.cloned.1.call-done
  1276.0 35.6 reduce-scatter.49.cloned.1.call-done
  1420.5 35.5 reduce-scatter.67.cloned.1.call-done
  1456.0 35.8 reduce-scatter.59.cloned.1.call-done
  1675.9 35.6 reduce-scatter.61.cloned.1.call-done
  1711.5 35.6 reduce-scatter.53.cloned.1.call-done
  1963.0 33.5 reduce-scatter.89.cloned.1.call-done
  2036.4 31.4 reduce-scatter.71.cloned.1.call-done
  2067.8 35.6 reduce-scatter.55.cloned.1.call-done
  2200.1 32.5 reduce-scatter.83.cloned.1.call-done
  2234.6 33.7 reduce-scatter.99.cloned.1.call-done
  2427.6 33.7 reduce-scatter.85.cloned.1.call-done
  2463.3 34.1 reduce-scatter.101.cloned.1.call-done
  2861.7 52.5 %reduce-scatter.115.cloned.1.call-done = bf16[2,144,1152]{2,1,0:T(8,128)(2,1)} async-done(((bf16[2,1152,1152]{2,1,0:T(8,128)(2,1)}), bf16[2,144,1152]{2,1,0:T(8,128)(2,1)}) %reduce-scatter.115.cloned.1.call-update) | async-done | bytes 663568 | tf_op jit(solution)/shard_map/reduce_scatter | solution.py:352
  2914.1 107.1 %reduce-scatter.117.cloned.1.call-done = bf16[2,144,1152]{2,1,0:T(8,128)(2,1)} async-done(((bf16[2,1152,1152]{2,1,0:T(8,128)(2,1)}), bf16[2,144,1152]{2,1,0:T(8,128)(2,1)}) %reduce-scatter.117.cloned.1.call-update) | async-done | bytes 663568 | tf_op jit(solution)/shard_map/reduce_scatter | solution.py:352
  3024.4 104.0 %reduce-scatter.105.cloned.1.call-done = bf16[2,144,1152]{2,1,0:T(8,128)(2,1)} async-done(((bf16[2,1152,1152]{2,1,0:T(8,128)(2,1)}), bf16[2,144,1152]{2,1,0:T(8,128)(2,1)}) %reduce-scatter.105.cloned.1.call-update) | async-done | bytes 663568 | tf_op jit(solution)/shard_map/reduce_scatter | solution.py:349
  3128.4 107.0 %reduce-scatter.109.cloned.1.call-done = bf16[2,144,1152]{2,1,0:T(8,128)(2,1)} async-done(((bf16[2,1152,1152]{2,1,0:T(8,128)(2,1)}), bf16[2,144,1152]{2,1,0:T(8,128)(2,1)}) %reduce-scatter.109.cloned.1.call-update) | async-done | bytes 663568 | tf_op jit(solution)/shard_map/reduce_scatter | solution.py:349
  3235.4 107.1 %reduce-scatter.107.cloned.1.call-done = bf16[2,144,1152]{2,1,0:T(8,128)(2,1)} async-done(((bf16[2,1152,1152]{2,1,0:T(8,128)(2,1)}), bf16[2,144,1152]{2,1,0:T(8,128)(2,1)}) %reduce-scatter.107.cloned.1.call-update) | async-done | bytes 663568 | tf_op jit(solution)/shard_map/reduce_scatter | solution.py:349
  3342.5 107.2 %reduce-scatter.111.cloned.1.call-done = bf16[2,144,1152]{2,1,0:T(8,128)(2,1)} async-done(((bf16[2,1152,1152]{2,1,0:T(8,128)(2,1)}), bf16[2,144,1152]{2,1,0:T(8,128)(2,1)}) %reduce-scatter.111.cloned.1.call-update) | async-done | bytes 663568 | tf_op jit(solution)/shard_map/reduce_scatter | solution.py:349
  3452.9 32.1 reduce-scatter.95.cloned.1.call-done
  3485.0 36.2 reduce-scatter.87.cloned.1.call-done
  3521.2 35.8 reduce-scatter.103.cloned.1.call-done
  3559.9 40.3 all-reduce.8
  3619.5 650.4 %all-reduce.27.cloned.1.call-done = (bf16[2,1152,864]{2,0,1:T(2,128)(2,1)}, bf16[2,1152,864]{2,0,1:T(2,128)(2,1)}, bf16[2,1152,864]{2,0,1:T(2,128)(2,1)}, bf16[2...) async-done(((bf16[2,1152,864]{2,0,1:T(2,128)(2,1)}, ...) | async-done | bytes 21233680
  (1954 shorter events, 2157.6 us)
Async XLA Ops:
  64.0 188.8 %reduce-scatter.41.cloned.1.call-start = ((), (), s32[]{:S(2)}) async-start(), calls=%async_computation.58 | async-start | bytes 2949120 | tf_op jit(solution)/shard_map/reduce_scatter | solution.py:47
  144.0 135.2 %all-gather.113.cloned.1.call-start = ((), (), s32[]{:S(2)}) async-start(), calls=%async_computation.130 | async-start | bytes 2985984 | tf_op jit(solution)/shard_map/all_gather | solution.py:56
  146.3 136.8 %all-gather.49.cloned.1.call-start = ((), (), s32[]{:S(2)}) async-start(), calls=%async_computation.59 | async-start | bytes 1474560 | tf_op jit(solution)/shard_map/all_gather | solution.py:43
  433.3 187.1 %all-gather.115.cloned.1.call-start = ((), (), s32[]{:S(2)}) async-start(), calls=%async_computation.131 | async-start | bytes 2985984 | tf_op jit(solution)/shard_map/all_gather | solution.py:56
  433.9 186.5 %all-gather.55.cloned.1.call-start = ((), (), s32[]{:S(2)}) async-start(), calls=%async_computation.64 | async-start | bytes 1474560 | tf_op jit(solution)/shard_map/all_gather | solution.py:43
  476.5 149.4 %all-gather.81.cloned.1.call-start = ((), (), s32[]{:S(2)}) async-start(), calls=%async_computation.90 | async-start | bytes 1474560 | tf_op jit(solution)/shard_map/all_gather | solution.py:43
  524.3 135.5 %all-gather.117.cloned.1.call-start = ((), (), s32[]{:S(2)}) async-start(), calls=%async_computation.132 | async-start | bytes 2985984 | tf_op jit(solution)/shard_map/all_gather | solution.py:56
  558.6 191.3 %reduce-scatter.73.cloned.1.call-start = ((), (), s32[]{:S(2)}) async-start(), calls=%async_computation.91 | async-start | bytes 2949120 | tf_op jit(solution)/shard_map/reduce_scatter | solution.py:47
  842.3 120.0 %all-gather.119.cloned.1.call-start = ((), (), s32[]{:S(2)}) async-start(), calls=%async_computation.133 | async-start | bytes 2985984 | tf_op jit(solution)/shard_map/all_gather | solution.py:56
  1220.7 124.7 %all-gather.59.cloned.1.call-start = ((), (), s32[]{:S(2)}) async-start(), calls=%async_computation.68 | async-start | bytes 1474560 | tf_op jit(solution)/shard_map/all_gather | solution.py:43
  1373.8 118.0 %reduce-scatter.59.cloned.1.call-start = ((), (), s32[]{:S(2)}) async-start(), calls=%async_computation.77 | async-start | bytes 2949120 | tf_op jit(solution)/shard_map/reduce_scatter | solution.py:47
  1668.1 195.9 %all-gather.79.cloned.1.call-start = ((), (), s32[]{:S(2)}) async-start(), calls=%async_computation.88 | async-start | bytes 1474560 | tf_op jit(solution)/shard_map/all_gather | solution.py:43
  1913.8 118.3 %reduce-scatter.63.cloned.1.call-start = ((), (), s32[]{:S(2)}) async-start(), calls=%async_computation.81 | async-start | bytes 2949120 | tf_op jit(solution)/shard_map/reduce_scatter | solution.py:47
  1919.7 148.1 %reduce-scatter.71.cloned.1.call-start = ((), (), s32[]{:S(2)}) async-start(), calls=%async_computation.89 | async-start | bytes 2949120 | tf_op jit(solution)/shard_map/reduce_scatter | solution.py:47
  1925.6 177.8 %reduce-scatter.55.cloned.1.call-start = ((), (), s32[]{:S(2)}) async-start(), calls=%async_computation.73 | async-start | bytes 2949120 | tf_op jit(solution)/shard_map/reduce_scatter | solution.py:47
  1931.4 191.6 %all-gather.99.cloned.1.call-start = ((), (), s32[]{:S(2)}) async-start(), calls=%async_computation.108 | async-start | bytes 1474560 | tf_op jit(solution)/shard_map/all_gather | solution.py:43
  2035.7 116.9 %all-gather.91.cloned.1.call-start = ((), (), s32[]{:S(2)}) async-start(), calls=%async_computation.100 | async-start | bytes 1474560 | tf_op jit(solution)/shard_map/all_gather | solution.py:43
  2382.1 115.3 %reduce-scatter.101.cloned.1.call-start = ((), (), s32[]{:S(2)}) async-start(), calls=%async_computation.119 | async-start | bytes 2949120 | tf_op jit(solution)/shard_map/reduce_scatter | solution.py:47
  2401.2 189.4 %all-gather.103.cloned.1.call-start = ((), (), s32[]{:S(2)}) async-start(), calls=%async_computation.112 | async-start | bytes 1474560 | tf_op jit(solution)/shard_map/all_gather | solution.py:43
  2515.6 136.0 %all-gather.111.cloned.1.call-start = ((), (), s32[]{:S(2)}) async-start(), calls=%async_computation.120 | async-start | bytes 1474560 | tf_op jit(solution)/shard_map/all_gather | solution.py:43
  2518.5 343.1 %reduce-scatter.113.cloned.1.call-start = ((), (), s32[]{:S(2)}) async-start(), calls=%async_computation.126 | async-start | bytes 5971968 | tf_op jit(solution)/shard_map/reduce_scatter | solution.py:352
  2527.5 334.2 %reduce-scatter.119.cloned.1.call-start = ((), (), s32[]{:S(2)}) async-start(), calls=%async_computation.129 | async-start | bytes 5971968 | tf_op jit(solution)/shard_map/reduce_scatter | solution.py:352
  2537.2 376.9 %reduce-scatter.115.cloned.1.call-start = ((), (), s32[]{:S(2)}) async-start(), calls=%async_computation.127 | async-start | bytes 5971968 | tf_op jit(solution)/shard_map/reduce_scatter | solution.py:352
  2547.0 474.2 %reduce-scatter.117.cloned.1.call-start = ((), (), s32[]{:S(2)}) async-start(), calls=%async_computation.128 | async-start | bytes 5971968 | tf_op jit(solution)/shard_map/reduce_scatter | solution.py:352
  2556.6 571.7 %reduce-scatter.105.cloned.1.call-start = ((), (), s32[]{:S(2)}) async-start(), calls=%async_computation.122 | async-start | bytes 5971968 | tf_op jit(solution)/shard_map/reduce_scatter | solution.py:349
  2564.9 670.5 %reduce-scatter.109.cloned.1.call-start = ((), (), s32[]{:S(2)}) async-start(), calls=%async_computation.124 | async-start | bytes 5971968 | tf_op jit(solution)/shard_map/reduce_scatter | solution.py:349
  2573.2 769.3 %reduce-scatter.107.cloned.1.call-start = ((), (), s32[]{:S(2)}) async-start(), calls=%async_computation.123 | async-start | bytes 5971968 | tf_op jit(solution)/shard_map/reduce_scatter | solution.py:349
  2581.7 868.0 %reduce-scatter.111.cloned.1.call-start = ((), (), s32[]{:S(2)}) async-start(), calls=%async_computation.125 | async-start | bytes 5971968 | tf_op jit(solution)/shard_map/reduce_scatter | solution.py:349
  2589.9 895.1 %reduce-scatter.95.cloned.1.call-start = ((), (), s32[]{:S(2)}) async-start(), calls=%async_computation.113 | async-start | bytes 2949120 | tf_op jit(solution)/shard_map/reduce_scatter | solution.py:47
  2604.3 916.8 %reduce-scatter.87.cloned.1.call-start = ((), (), s32[]{:S(2)}) async-start(), calls=%async_computation.105 | async-start | bytes 2949120 | tf_op jit(solution)/shard_map/reduce_scatter | solution.py:47
  2618.8 938.2 %reduce-scatter.103.cloned.1.call-start = ((), (), s32[]{:S(2)}) async-start(), calls=%async_computation.121 | async-start | bytes 2949120 | tf_op jit(solution)/shard_map/reduce_scatter | solution.py:47
  2665.7 1604.1 %all-reduce.27.cloned.1.call-start = ((), (), s32[]{:S(2)}) async-start(), calls=%async_computation.134 | async-start | bytes 47185920
  (545 other events, 22268.3 us)
Sparse Core Ops, SparseCore 0:
  79.3 53.0 all-gather.46
  178.6 82.1 all-gather.112
  327.4 61.1 all-gather.52
  468.8 61.8 all-gather.114
  532.3 51.0 all-gather.54
  604.7 55.0 all-gather.116
  712.6 34.8 reduce-scatter.46
  842.4 34.1 reduce-scatter.74
  878.6 77.0 all-gather.118
  988.6 33.0 reduce-scatter.76
  1100.4 33.0 reduce-scatter.78
  1207.3 33.0 reduce-scatter.56
  1278.5 33.0 reduce-scatter.48
  1387.4 33.0 reduce-scatter.50
  1458.7 33.0 reduce-scatter.58
  1642.8 33.0 reduce-scatter.68
  1714.1 33.0 reduce-scatter.52
  1927.8 33.0 reduce-scatter.80
  2070.3 33.0 reduce-scatter.54
  2163.9 33.0 reduce-scatter.90
  2199.6 33.0 reduce-scatter.82
  2235.2 33.0 reduce-scatter.98
  2573.8 103.9 reduce-scatter.112
  2682.0 116.2 reduce-scatter.118
  2802.3 111.7 reduce-scatter.114
  2918.3 102.9 reduce-scatter.116
  3025.3 103.0 reduce-scatter.104
  3132.4 102.9 reduce-scatter.108
  3239.4 103.0 reduce-scatter.106
  3346.6 103.0 reduce-scatter.110
  3523.9 33.0 reduce-scatter.102
  3562.7 707.1 all-reduce.26
  (47 shorter events, 1060.6 us)
